TPU v7x, 256 devices: a whole 4x4x8 slice. The times are simulated.
256 devices in a mesh: rep: 2 (over z_hi), dp: 32 (over z_lo, x, core), mp: 4 (over y).
Axes of the slice: x: 4, y: 4, z: 8 (z_hi: 2, z_lo: 4; z = z_hi * 4 + z_lo), core: 2. Of those that a mesh axis runs over, the one named last changes fastest.
Arguments:
- tokens: bfloat16 [24576, 2048], P(('rep', 'dp', 'mp')), may hold values from -6 to 6
- request_ids: int32 [64, 384], P(('rep', 'dp')), may hold values from 0 to 7, never falling along the last dimension, each value on 1 to 192 neighbouring positions
- cache_entries: bfloat16 [32768, 4096], P(('rep', 'dp', 'mp')), may hold values from -250 to 250, as said below
- cached_lengths: int32 [64, 8], replicated, may hold values from 1 to 256, 512 in all within a row
- traded: int32 [32], P('dp'), may hold values from 0 to 1, as said below
- query_weight: bfloat16 [2048, 2048], P(None, 'mp'), may hold values from -0.125 to 0.125
- key_weight: bfloat16 [2048, 2048], P(None, 'mp'), may hold values from -0.125 to 0.125
- value_weight: bfloat16 [2048, 2048], P(None, 'mp'), may hold values from -0.125 to 0.125
- output_weight: bfloat16 [2048, 2048], P('mp'), may hold values from -0.125 to 0.125
- gate_weight: bfloat16 [2048, 8192], P('dp', 'mp'), may hold values from -0.125 to 0.125
- up_weight: bfloat16 [2048, 8192], P('dp', 'mp'), may hold values from -0.125 to 0.125
- down_weight: bfloat16 [2048, 8192], P('dp', 'mp'), may hold values from -0.0625 to 0.0625
Outputs:
- layer_output: bfloat16 [24576, 2048], P(('rep', 'dp', 'mp'))
Inputs may be any that keep to these rules, and one draw needn't show every extreme that they name: `request_ids`: each group's row never falls; every request 0 to 7 has 1 to 192 new tokens in each group, some request exactly 192. `cached_lengths`: each row sums to 512; its largest entry is 256. `traded`: exactly 16 entries are 1. `cache_entries`: keys are stored already rotated to their positions; rows of cache group g are g * 512 to (g + 1) * 512 - 1, the requests' prefixes in request order.
All inputs are finite; a program needn't handle non-finite values.
Results may differ from a plain program's by a relative error of at most 0.013.
The roundings to bfloat16 on the way count: a program that leaves them out, or rounds other values in their place, can miss the bound.
Values may be sent and summed in bfloat16 or wider, within the bound.
A program may use at most 128 MiB of HBM per device.

v0:
```python
import math
import jax
import jax.numpy as jnp
from jax import lax
from jax.sharding import PartitionSpec as P

D = 2048
HEADS = 16
HEAD_DIM = 128
TOK_GROUP = 384
CACHE = 512
EPSILON = 1e-05
ROPE_BASE = 10000.0


def swapped(value, axis, apart):
    mask = 2**apart
    pairs = [(source, source ^ mask) for source in range(lax.axis_size(axis))]
    return lax.ppermute(value, axis, pairs)


def layer_norm(rows):
    center = rows - jnp.mean(rows, axis=-1, keepdims=True)
    spread = jnp.mean(center * center, axis=-1, keepdims=True)
    return center * lax.rsqrt(spread + EPSILON)


def request_layout(request_row, length_row, cache_size):
    number = length_row.shape[0]
    labels = jnp.arange(number, dtype=jnp.int32)
    onehot = (request_row[:, None] == labels[None, :]).astype(jnp.int32)
    counts = jnp.sum(onehot, axis=0)
    starts = jnp.cumsum(counts) - counts
    token_place = jnp.arange(request_row.shape[0], dtype=jnp.int32)
    positions = jnp.sum(onehot * (length_row - starts)[None, :], axis=1) + token_place
    bounds = jnp.cumsum(length_row)
    cache_place = jnp.arange(cache_size, dtype=jnp.int32)
    owner = jnp.sum((cache_place[:, None] >= bounds[None, :]).astype(jnp.int32), axis=1)
    return (positions, owner)


def rotate(vectors, positions):
    half = vectors.shape[-1] // 2
    freq = ROPE_BASE ** (-jnp.arange(half, dtype=jnp.float32) / half)
    angle = positions.astype(jnp.float32)[:, None] * freq[None, :]
    cosine = jnp.cos(angle)[:, None, :]
    sine = jnp.sin(angle)[:, None, :]
    first = vectors[..., :half]
    second = vectors[..., half:]
    return jnp.concatenate(
        [first * cosine - second * sine, second * cosine + first * sine], axis=-1
    )


def attend(query, keys_new, values_new, keys_cache, values_cache, request_row, owner):
    scale = 1.0 / math.sqrt(query.shape[-1])
    keys = jnp.concatenate([keys_cache, keys_new], axis=0)
    values = jnp.concatenate([values_cache, values_new], axis=0)
    scores = jnp.einsum("thd,khd->htk", query, keys, preferred_element_type=jnp.float32) * scale
    count = request_row.shape[0]
    place = jnp.arange(count, dtype=jnp.int32)
    same_cache = owner[None, :] == request_row[:, None]
    same_new = (request_row[None, :] == request_row[:, None]) & (place[None, :] <= place[:, None])
    allowed = jnp.concatenate([same_cache, same_new], axis=1)
    scores = jnp.where(allowed[None], scores, -1e30)
    top = jnp.max(scores, axis=-1, keepdims=True)
    raised = jnp.exp(scores - top)
    total = jnp.sum(raised, axis=-1, keepdims=True)
    weights = (raised / total).astype(jnp.bfloat16)
    mixed = jnp.einsum("htk,khd->thd", weights, values, preferred_element_type=jnp.float32)
    return mixed.astype(jnp.bfloat16)


def local(
    tokens,
    request_ids,
    cache_entries,
    cached_lengths,
    traded,
    query_weight,
    key_weight,
    value_weight,
    output_weight,
    gate_weight,
    up_weight,
    down_weight,
):
    tensor_size = lax.axis_size("mp")
    local_heads = HEADS // tensor_size
    replica = lax.axis_index("rep")
    within = lax.axis_index("dp")
    pairs = lax.axis_size("dp")
    group = replica * pairs + within
    moved_here = traded[0] == 1
    source = jnp.where(moved_here, (1 - replica) * pairs + within, group)
    length_row = lax.dynamic_slice_in_dim(cached_lengths, source, 1, 0)[0]
    request_row = request_ids[0]
    partner = swapped(cache_entries, "rep", 0)
    stored = jnp.where(moved_here, partner, cache_entries)
    by_heads = lax.all_to_all(
        stored.reshape(stored.shape[0], 2, D), "mp", split_axis=2, concat_axis=0, tiled=True
    )
    keys_cache = by_heads[:, 0].reshape(CACHE, local_heads, HEAD_DIM)
    values_cache = by_heads[:, 1].reshape(CACHE, local_heads, HEAD_DIM)
    rows_full = lax.all_gather(tokens, "mp", axis=0, tiled=True)
    positions, owner = request_layout(request_row, length_row, CACHE)
    normed = layer_norm(rows_full.astype(jnp.float32)).astype(jnp.bfloat16)
    query = jnp.dot(normed, query_weight, preferred_element_type=jnp.float32).reshape(
        TOK_GROUP, local_heads, HEAD_DIM
    )
    query = rotate(query, positions).astype(jnp.bfloat16)
    keys_new = jnp.dot(normed, key_weight, preferred_element_type=jnp.float32).reshape(
        TOK_GROUP, local_heads, HEAD_DIM
    )
    keys_new = rotate(keys_new, positions).astype(jnp.bfloat16)
    values_new = (
        jnp.dot(normed, value_weight, preferred_element_type=jnp.float32)
        .astype(jnp.bfloat16)
        .reshape(TOK_GROUP, local_heads, HEAD_DIM)
    )
    mixed = attend(query, keys_new, values_new, keys_cache, values_cache, request_row, owner)
    mixed = mixed.reshape(TOK_GROUP, local_heads * HEAD_DIM)
    own_sum = lax.psum_scatter(
        jnp.dot(mixed, output_weight, preferred_element_type=jnp.float32),
        "mp",
        scatter_dimension=0,
        tiled=True,
    )
    state_own = (tokens.astype(jnp.float32) + own_sum).astype(jnp.bfloat16)
    normed_own = layer_norm(state_own.astype(jnp.float32)).astype(jnp.bfloat16)
    normed_two = lax.all_gather(normed_own, "mp", axis=0, tiled=True)

    def add_rows(piece):
        return jnp.dot(normed_two, piece, preferred_element_type=jnp.float32)

    gate = add_rows(lax.all_gather(gate_weight, "dp", axis=0, tiled=True))
    upward = add_rows(lax.all_gather(up_weight, "dp", axis=0, tiled=True))
    activated = (jax.nn.silu(gate) * upward).astype(jnp.bfloat16)
    terms = lax.dot_general(
        activated,
        lax.all_gather(down_weight, "dp", axis=0, tiled=True),
        (((1,), (1,)), ((), ())),
        preferred_element_type=jnp.float32,
    )
    hidden_own = lax.psum_scatter(terms, "mp", scatter_dimension=0, tiled=True)
    return (state_own.astype(jnp.float32) + hidden_own).astype(jnp.bfloat16)


def solution(mesh):
    in_specs = (
        P(("rep", "dp", "mp"), None),
        P(("rep", "dp"), None),
        P(("rep", "dp", "mp"), None),
        P(),
        P("dp"),
        P(None, "mp"),
        P(None, "mp"),
        P(None, "mp"),
        P("mp", None),
        P("dp", "mp"),
        P("dp", "mp"),
        P("dp", "mp"),
    )
    out_specs = P(("rep", "dp", "mp"), None)
    return jax.shard_map(local, mesh=mesh, in_specs=in_specs, out_specs=out_specs, check_vma=False)
```

profile of v0, /device:TPU:1, one launch (start us, length us, event | category | flops | bytes accessed | tf_op | source)
XLA Modules:
  0.0 476.3 jit_solution(9177185737929228484)
XLA Ops:
  6.5 1.8 copy.71
  8.3 7.8 %collective-permute-start = (bf16[128,4096]{0,1:T(8,128)(2,1)S(1)}, bf16[128,4096]{0,1:T(8,128)(2,1)}, u32[]{:S(2)}, u32[]{:S(2)}) collective-permute-start(bf16[128,4096]{0,1:T(8,128)(2,1)S(1)} %copy.71), channel_id=1, source_target_pairs={{0,128},{128,0},{1,129},{129,1},{2,130},{130,2},{3,131},{131,3},{4... | collective-permute-start | bytes 3145736 | tf_op jit(solution)/shard_map/ppermute | solution.py:19
  16.1 0.0 all-gather.6.cloned.1.call-update
  16.8 0.8 constant_dynamic-slice_fusion
  17.6 0.1 copy.86
  17.7 0.7 reduce
  18.4 0.1 convert_reduce_fusion.3
  18.5 0.2 reduce-window_1_clone.1
  18.7 0.2 reduce-window.9
  18.8 0.1 convert_reduce_fusion.2
  18.9 0.1 select_reduce_fusion
  19.0 0.2 broadcast_compare_fusion
  19.2 25.3 %collective-permute-done = bf16[128,4096]{0,1:T(8,128)(2,1)} collective-permute-done((bf16[128,4096]{0,1:T(8,128)(2,1)S(1)}, bf16[128,4096]{0,1:T(8,128)(2,1)}, u32[]{:S(2)}, u32[]{:S(2)}) %collective-permute-start) | collective-permute-done | bytes 1048608 | tf_op jit(solution)/shard_map/ppermute | solution.py:19
  44.6 1.3 broadcast_select_fusion
  45.9 9.5 %copy.73 = bf16[128,2,2048]{0,1,2:T(2,128)(2,1)} copy(bf16[128,2,2048]{0,2,1:T(8,128)(2,1)S(1)} %bitcast.28) | data formatting | bytes 2097152 | tf_op jit(solution)/shard_map/reshape | solution.py:101
  55.4 4.7 all-to-all-start
  60.1 0.1 fusion.26
  60.2 0.8 pad_add_fusion
  61.0 1.5 multiply_cosine_fusion
  62.5 7.3 %all-to-all-done = bf16[128,2,2048]{0,1,2:T(2,128)(2,1)S(1)} async-done(((bf16[128,2,2048]{0,1,2:T(2,128)(2,1)}), bf16[128,2,2048]{0,1,2:T(2,128)(2,1)S(1)}, u32[]{:S(2)}, u32[]{:S(2)}) %all-to-all-start) | async-done | bytes 1048608 | tf_op jit(solution)/shard_map/all_to_all | solution.py:100
  69.8 1.1 copy.74
  70.9 1.5 copy.75
  72.4 1.0 fusion.40
  73.5 1.3 copy.81
  74.7 0.3 copy.84
  75.0 2.0 copy.76
  77.0 1.8 convert_reduce_fusion
  78.9 2.0 fusion.4
  80.8 3.6 fusion.35
  84.4 1.4 reshape.153
  85.8 4.0 fusion.37
  89.8 2.3 reshape.151
  92.1 3.9 convolution_convert_fusion
  95.9 1.9 copy.85
  97.8 2.3 fusion.41
  100.2 0.4 subtract_convert_fusion.1
  100.6 0.9 fusion.16
  101.5 0.0 copy-done.8
  101.6 2.7 fusion.43
  104.3 1.1 fusion.10
  105.4 2.7 fusion.44
  108.1 0.0 reduce-scatter.3.cloned.1.call-update
  108.1 0.3 all-gather.8.cloned.1.call-start
  108.4 61.6 %reduce-scatter.3.cloned.1.call-done = f32[96,2048]{1,0:T(8,128)} async-done(((f32[384,2048]{1,0:T(8,128)}), f32[96,2048]{1,0:T(8,128)}) %reduce-scatter.3.cloned.1.call-update) | async-done | bytes 786448 | tf_op jit(solution)/shard_map/reduce_scatter | solution.py:123
  169.9 1.3 convert_reduce_fusion.1
  171.3 0.3 fusion.22
  171.6 1.0 fusion.23
  172.5 0.0 all-gather.8.cloned.1.call-update
  172.6 0.0 all-gather.10.cloned.1.call-start
  172.6 0.5 all-gather.10.cloned.1.call-update
  173.1 0.0 all-gather.12.cloned.1.call-start
  173.2 0.5 all-gather.12.cloned.1.call-update
  173.7 0.0 all-gather.14.cloned.1.call-start
  173.8 0.5 all-gather.14.cloned.1.call-update
  174.3 0.0 reduce-scatter.5.cloned.1.call-start
  174.4 27.1 %all-gather.8.cloned.1.call-done = bf16[384,2048]{1,0:T(8,128)(2,1)} async-done(((bf16[96,2048]{1,0:T(8,128)(2,1)}), bf16[384,2048]{1,0:T(8,128)(2,1)}) %all-gather.8.cloned.1.call-update) | async-done | bytes 1572880 | tf_op jit(solution)/shard_map/all_gather | solution.py:131
  201.5 71.4 %all-gather.10.cloned.1.call-done = bf16[2048,2048]{1,0:T(8,128)(2,1)} async-done(((bf16[64,2048]{1,0:T(8,128)(2,1)}), bf16[2048,2048]{1,0:T(8,128)(2,1)}) %all-gather.10.cloned.1.call-update) | async-done | bytes 8388624 | tf_op jit(solution)/shard_map/all_gather | solution.py:136
  272.9 9.0 %fusion.45 = f32[384,2048]{1,0:T(8,128)} fusion(bf16[384,2048]{1,0:T(8,128)(2,1)} %all-gather.8.cloned.1.call-done, bf16[2048,2048]{1,0:T(8,128)(2,1)} %all-gather.10.cloned.1.call-done), kind=kOutput, calls=%fused_computation.76 | convolution fusion | flops 3221225472 | bytes 13107200 | tf_op jit(solution)/shard_map/dot_general | solution.py:134
  281.9 60.6 %all-gather.12.cloned.1.call-done = bf16[2048,2048]{1,0:T(8,128)(2,1)} async-done(((bf16[64,2048]{1,0:T(8,128)(2,1)}), bf16[2048,2048]{1,0:T(8,128)(2,1)}) %all-gather.12.cloned.1.call-update) | async-done | bytes 8388624 | tf_op jit(solution)/shard_map/all_gather | solution.py:137
  342.5 69.7 %all-gather.14.cloned.1.call-done = bf16[2048,2048]{1,0:T(8,128)(2,1)} async-done(((bf16[64,2048]{1,0:T(8,128)(2,1)}), bf16[2048,2048]{1,0:T(8,128)(2,1)}) %all-gather.14.cloned.1.call-update) | async-done | bytes 8388624 | tf_op jit(solution)/shard_map/all_gather | solution.py:141
  412.2 15.9 %fusion.25 = f32[384,2048]{1,0:T(8,128)} fusion(bf16[2048,2048]{1,0:T(8,128)(2,1)} %all-gather.14.cloned.1.call-done, f32[384,2048]{1,0:T(8,128)} %fusion.45, bf16[384,2048]{1,0:T(8,128)(2,1)} %all-gather.8.cloned.1.call-done, bf16[2048,2048]{1,0:T(8,128)(2,1)} %all-gather.12.cloned.1.call-done), kind=kOutput, calls=%fused_computation.42 | convolution fusion | flops 6447169536 | bytes 24641536 | tf_op jit(solution)/shard_map/dot_general | solution.py:139
  428.1 0.0 reduce-scatter.5.cloned.1.call-update
  428.1 39.4 %reduce-scatter.5.cloned.1.call-done = f32[96,2048]{1,0:T(8,128)} async-done(((f32[384,2048]{1,0:T(8,128)}), f32[96,2048]{1,0:T(8,128)}) %reduce-scatter.5.cloned.1.call-update) | async-done | bytes 786448 | tf_op jit(solution)/shard_map/reduce_scatter | solution.py:145
  467.5 2.0 fusion.24
  (27 shorter events, 0.1 us)
Async XLA Ops:
  6.5 98.8 %copy-start = (bf16[512,2048]{1,0:T(8,128)(2,1)S(1)}, bf16[512,2048]{1,0:T(8,128)(2,1)}, u32[]{:S(2)}) copy-start(bf16[512,2048]{1,0:T(8,128)(2,1)} %param.20) | copy-start | bytes 6291460
  6.5 70.5 %all-gather.6.cloned.1.call-start = ((), (), s32[]{:S(2)}) async-start(), calls=%async_computation.3 | async-start | bytes 1966080 | tf_op jit(solution)/shard_map/all_gather | solution.py:105
  8.3 36.3 %collective-permute-start = (bf16[128,4096]{0,1:T(8,128)(2,1)S(1)}, bf16[128,4096]{0,1:T(8,128)(2,1)}, u32[]{:S(2)}, u32[]{:S(2)}) collective-permute-start(bf16[128,4096]{0,1:T(8,128)(2,1)S(1)} %copy.71), channel_id=1, source_target_pairs={{0,128},{128,0},{1,129},{129,1},{2,130},{130,2},{3,131},{131,3},{4... | collective-permute-start | bytes 3145736 | tf_op jit(solution)/shard_map/ppermute | solution.py:19
  55.4 14.5 %all-to-all-start = ((bf16[128,2,2048]{0,1,2:T(2,128)(2,1)}), bf16[128,2,2048]{0,1,2:T(2,128)(2,1)S(1)}, u32[]{:S(2)}, u32[]{:S(2)}) async-start(bf16[128,2,2048]{0,1,2:T(2,128)(2,1)} %copy.73), calls=%async_computation | async-start | bytes 2097152 | tf_op jit(solution)/shard_map/all_to_all | solution.py:100
  60.1 109.8 %reduce-scatter.3.cloned.1.call-start = ((), (), s32[]{:S(2)}) async-start(), calls=%async_computation.4 | async-start | bytes 3932160 | tf_op jit(solution)/shard_map/reduce_scatter | solution.py:123
  77.0 3.8 copy-start.2
  97.8 2.3 copy-start.4
  97.8 2.3 copy-start.5
  100.6 1.0 copy-start.8
  101.6 2.7 copy-start.6
  101.6 2.7 copy-start.7
  105.4 64.5 %copy-start.3 = (bf16[96,2048]{1,0:T(8,128)(2,1)S(1)}, bf16[96,2048]{1,0:T(8,128)(2,1)}, u32[]{:S(2)}) copy-start(bf16[96,2048]{1,0:T(8,128)(2,1)} %param.12) | copy-start | bytes 1179652
  108.1 93.4 %all-gather.8.cloned.1.call-start = ((), (), s32[]{:S(2)}) async-start(), calls=%async_computation.5 | async-start | bytes 1966080 | tf_op jit(solution)/shard_map/all_gather | solution.py:131
  172.6 100.3 %all-gather.10.cloned.1.call-start = ((), (), s32[]{:S(2)}) async-start(), calls=%async_computation.6 | async-start | bytes 8650752 | tf_op jit(solution)/shard_map/all_gather | solution.py:136
  173.1 169.4 %all-gather.12.cloned.1.call-start = ((), (), s32[]{:S(2)}) async-start(), calls=%async_computation.7 | async-start | bytes 8650752 | tf_op jit(solution)/shard_map/all_gather | solution.py:137
  173.7 238.5 %all-gather.14.cloned.1.call-start = ((), (), s32[]{:S(2)}) async-start(), calls=%async_computation.8 | async-start | bytes 8650752 | tf_op jit(solution)/shard_map/all_gather | solution.py:141
  174.3 293.2 %reduce-scatter.5.cloned.1.call-start = ((), (), s32[]{:S(2)}) async-start(), calls=%async_computation.9 | async-start | bytes 3932160 | tf_op jit(solution)/shard_map/reduce_scatter | solution.py:145
  412.2 57.2 %copy-start.1 = (bf16[512,2048]{1,0:T(8,128)(2,1)S(1)}, bf16[512,2048]{1,0:T(8,128)(2,1)}, u32[]{:S(2)}) copy-start(bf16[512,2048]{1,0:T(8,128)(2,1)} %param.20) | copy-start | bytes 6291460
Sparse Core Ops, SparseCore 0:
  16.3 27.0 all-gather.5
  108.2 61.6 reduce-scatter.2
  172.7 28.7 all-gather.7
  203.2 69.6 all-gather.9
  274.6 67.9 all-gather.11
  344.2 67.9 all-gather.13
  428.2 39.2 reduce-scatter.4
where the time goes:
time: 477 us; the launch traced here: 476 us
  waiting for transfers between devices  364 us (76%)
  matrix products  41 us (9%)
  local copies, waits for them, and re-layouts  27.2 us (6%)
  other arithmetic  16.8 us (4%)
  between operations  14.3 us (3%)
  starting transfers between devices  13 us (3%)
    all_gather x1, waiting for transfers between devices, local(): gate = add_rows(lax.all_gather(gate_weight, 'dp', axis=0, tiled=True))  71.4 us
    all_gather x1, waiting for transfers between devices, local(): lax.all_gather(down_weight, 'dp', axis=0, tiled=True)  69.7 us
    reduce_scatter x1, waiting for transfers between devices, local(): lax.psum_scatter(jnp.dot(mixed, output_weight, preferred_element_type=jnp...  61.6 us
    all_gather x1, waiting for transfers between devices, local(): upward = add_rows(lax.all_gather(up_weight, 'dp', axis=0, tiled=True))  60.6 us
    reduce_scatter x1, waiting for transfers between devices, local(): hidden_own = lax.psum_scatter(terms, 'mp', scatter_dimension=0, tiled=True)  39.4 us
    all_gather x1, waiting for transfers between devices, local(): normed_two = lax.all_gather(normed_own, 'mp', axis=0, tiled=True)  27.1 us
    ppermute x1, waiting for transfers between devices, swapped(): return lax.ppermute(value, axis, pairs)  25.3 us
    dot_general x1, matrix products, local(): lax.dot_general(activated, lax.all_gather(down_weight, 'dp', axis=0, tile...  15.9 us
  transfers between devices with their start and end apart: 9, of which 8 were waited for; matrix products, arithmetic and copies ran while one was open for 7% of the time, Pallas kernels for 0%

commit v1 on v0

--- a/solution.py
+++ b/solution.py
@@ -1,8 +1,10 @@
+import functools
 import math
 import jax
 import jax.numpy as jnp
 from jax import lax
 from jax.sharding import PartitionSpec as P
+from jax.lax import axis_index, axis_size, ppermute
 
 D = 2048
 HEADS = 16
@@ -11,6 +13,33 @@
 CACHE = 512
 EPSILON = 1e-05
 ROPE_BASE = 10000.0
+
+
+def lift_the_packet(x_part, k_dim):
+    back = axis_size("mp")
+    placed, carry_out, spare = (back, axis_index("mp"), x_part.shape[k_dim])
+    store = [d * placed if num == k_dim else d for num, d in enumerate(x_part.shape)]
+    s_next = jnp.zeros(store, x_part.dtype)
+    all_rows = block_now = x_part
+    reply = lax.dynamic_update_slice_in_dim(s_next, x_part, carry_out * spare, axis=k_dim)
+    for nth in range(1, placed // 2 + 1):
+        all_rows = ppermute(
+            all_rows, axis_name="mp", perm=[(num, (num + 1) % placed) for num in range(placed)]
+        )
+        reply = lax.dynamic_update_slice_in_dim(
+            reply, all_rows, (carry_out - nth) % placed * spare, axis=k_dim
+        )
+        if 2 * nth < placed:
+            block_now = ppermute(
+                block_now, axis_name="mp", perm=[(num, (num - 1) % placed) for num in range(placed)]
+            )
+            reply = lax.dynamic_update_slice_in_dim(
+                reply, block_now, (carry_out + nth) % placed * spare, axis=k_dim
+            )
+    return reply
+
+
+change_the_columns = functools.partial(lift_the_packet, k_dim=0)
 
 
 def swapped(value, axis, apart):
@@ -128,7 +157,7 @@
     )
     state_own = (tokens.astype(jnp.float32) + own_sum).astype(jnp.bfloat16)
     normed_own = layer_norm(state_own.astype(jnp.float32)).astype(jnp.bfloat16)
-    normed_two = lax.all_gather(normed_own, "mp", axis=0, tiled=True)
+    normed_two = change_the_columns(normed_own)
 
     def add_rows(piece):
         return jnp.dot(normed_two, piece, preferred_element_type=jnp.float32)

time: 477 us -> 409 us (0.86)
  waiting for transfers between devices: 364 us -> 293 us
    all_gather x1, waiting for transfers between devices: 71.4 us -> 7.62 us  [local(): gate = add_rows(lax.all_gather(gate_weight, 'dp', axis=0, tiled=True))]
    all_gather x1 -> x0, waiting for transfers between devices: 27.1 us -> none  [local(): normed_two = lax.all_gather(normed_own, 'mp', axis=0, tiled=True)]
    ppermute x0 -> x3, waiting for transfers between devices: none -> 18.8 us  [the longest x2 18.8 us: lift_the_packet(): ppermute(all_rows, axis_name='mp', perm=[(num, (num + 1) % placed) for nu...]
    all_gather x1, waiting for transfers between devices: 60.6 us -> 70.6 us  [local(): upward = add_rows(lax.all_gather(up_weight, 'dp', axis=0, tiled=True))]
    all_gather x1, waiting for transfers between devices: 69.7 us -> 61.8 us  [local(): lax.all_gather(down_weight, 'dp', axis=0, tiled=True)]
  transfers between devices with their start and end apart: 9 -> 11, of which waited for: 8 -> 9; matrix products, arithmetic and copies ran while one was open for 7% -> 8% of each run, Pallas kernels for 0% -> 0%
where the time goes in v1:
time: 409 us; the launch traced here: 408 us
  waiting for transfers between devices  293 us (72%)
  matrix products  40.6 us (10%)
  local copies, waits for them, and re-layouts  27.5 us (7%)
  other arithmetic  16 us (4%)
  starting transfers between devices  15.7 us (4%)
  between operations  15.7 us (4%)
    all_gather x1, waiting for transfers between devices, local(): upward = add_rows(lax.all_gather(up_weight, 'dp', axis=0, tiled=True))  70.6 us
    all_gather x1, waiting for transfers between devices, local(): lax.all_gather(down_weight, 'dp', axis=0, tiled=True)  61.8 us
    reduce_scatter x1, waiting for transfers between devices, local(): lax.psum_scatter(jnp.dot(mixed, output_weight, preferred_element_type=jnp...  59.8 us
    reduce_scatter x1, waiting for transfers between devices, local(): hidden_own = lax.psum_scatter(terms, 'mp', scatter_dimension=0, tiled=True)  40 us
    ppermute x1, waiting for transfers between devices, swapped(): return lax.ppermute(value, axis, pairs)  25.3 us
    ppermute x2, waiting for transfers between devices, lift_the_packet(): ppermute(all_rows, axis_name='mp', perm=[(num, (num + 1) % placed) for nu...  18.8 us
    dot_general x1, matrix products, local(): lax.dot_general(activated, lax.all_gather(down_weight, 'dp', axis=0, tile...  15.9 us
    reshape x1, local copies, waits for them, and re-layouts, local(): stored.reshape(stored.shape[0], 2, D)  9.46 us
  transfers between devices with their start and end apart: 11, of which 9 were waited for; matrix products, arithmetic and copies ran while one was open for 8% of the time, Pallas kernels for 0%

profile of v1, /device:TPU:1, one launch (start us, length us, event | category | flops | bytes accessed | tf_op | source)
XLA Modules:
  0.0 408.4 jit_solution(12269917901234225970)
XLA Ops:
  7.4 1.8 copy.71
  9.1 7.8 %collective-permute-start = (bf16[128,4096]{0,1:T(8,128)(2,1)S(1)}, bf16[128,4096]{0,1:T(8,128)(2,1)}, u32[]{:S(2)}, u32[]{:S(2)}) collective-permute-start(bf16[128,4096]{0,1:T(8,128)(2,1)S(1)} %copy.71), channel_id=1, source_target_pairs={{0,128},{128,0},{1,129},{129,1},{2,130},{130,2},{3,131},{131,3},{4... | collective-permute-start | bytes 3145736 | tf_op jit(solution)/shard_map/ppermute | solution.py:48
  17.0 0.0 all-gather.5.cloned.1.call-update
  17.7 0.8 constant_dynamic-slice_fusion
  18.4 0.1 copy.86
  18.5 0.7 reduce
  19.2 0.1 convert_reduce_fusion.3
  19.3 0.2 reduce-window_1_clone.1
  19.5 0.2 reduce-window.9
  19.7 0.1 convert_reduce_fusion.2
  19.8 0.1 select_reduce_fusion
  19.9 0.2 broadcast_compare_fusion
  20.1 25.3 %collective-permute-done = bf16[128,4096]{0,1:T(8,128)(2,1)} collective-permute-done((bf16[128,4096]{0,1:T(8,128)(2,1)S(1)}, bf16[128,4096]{0,1:T(8,128)(2,1)}, u32[]{:S(2)}, u32[]{:S(2)}) %collective-permute-start) | collective-permute-done | bytes 1048608 | tf_op jit(solution)/shard_map/ppermute | solution.py:48
  45.4 1.3 broadcast_select_fusion
  46.7 9.5 %copy.73 = bf16[128,2,2048]{0,1,2:T(2,128)(2,1)} copy(bf16[128,2,2048]{0,2,1:T(8,128)(2,1)S(1)} %bitcast.28) | data formatting | bytes 2097152 | tf_op jit(solution)/shard_map/reshape | solution.py:130
  56.2 4.7 %all-to-all-start = ((bf16[128,2,2048]{0,1,2:T(2,128)(2,1)}), bf16[128,2,2048]{0,1,2:T(2,128)(2,1)S(1)}, u32[]{:S(2)}, u32[]{:S(2)}) async-start(bf16[128,2,2048]{0,1,2:T(2,128)(2,1)} %copy.73), calls=%async_computation | async-start | bytes 2097152 | tf_op jit(solution)/shard_map/all_to_all | solution.py:129
  60.9 0.1 fusion.27
  61.1 0.8 pad_add_fusion
  61.8 1.5 multiply_cosine_fusion
  63.3 7.3 %all-to-all-done = bf16[128,2,2048]{0,1,2:T(2,128)(2,1)S(1)} async-done(((bf16[128,2,2048]{0,1,2:T(2,128)(2,1)}), bf16[128,2,2048]{0,1,2:T(2,128)(2,1)S(1)}, u32[]{:S(2)}, u32[]{:S(2)}) %all-to-all-start) | async-done | bytes 1048608 | tf_op jit(solution)/shard_map/all_to_all | solution.py:129
  70.7 1.1 copy.74
  71.8 1.5 copy.75
  73.3 1.0 fusion.42
  74.3 1.3 copy.81
  75.5 0.3 copy.84
  75.8 2.0 copy.76
  77.9 1.8 convert_reduce_fusion
  79.7 2.0 fusion.4
  81.7 3.5 fusion.38
  85.2 1.4 reshape.151
  86.6 4.0 fusion.36
  90.6 2.3 reshape.153
  92.9 3.9 convolution_convert_fusion
  96.7 1.9 copy.85
  98.7 2.3 fusion.43
  101.0 0.4 subtract_convert_fusion.1
  101.4 0.9 fusion.18
  102.4 0.0 copy-done.9
  102.4 2.7 fusion.45
  105.2 1.1 fusion.12
  106.2 2.8 fusion.48
  109.0 0.0 all-gather.7.cloned.1.call-start
  109.1 0.5 all-gather.7.cloned.1.call-update
  109.6 0.0 all-gather.11.cloned.1.call-start
  109.7 0.5 all-gather.11.cloned.1.call-update
  110.2 0.0 all-gather.9.cloned.1.call-start
  110.2 0.5 all-gather.9.cloned.1.call-update
  110.8 0.3 reduce-scatter.5.cloned.1.call-start
  111.0 59.8 %reduce-scatter.3.cloned.1.call-done = f32[96,2048]{1,0:T(8,128)} async-done(((f32[384,2048]{1,0:T(8,128)}), f32[96,2048]{1,0:T(8,128)}) %reduce-scatter.3.cloned.1.call-update) | async-done | bytes 786448 | tf_op jit(solution)/shard_map/reduce_scatter | solution.py:152
  170.8 1.3 convert_reduce_fusion.1
  172.2 0.3 fusion.24
  172.5 0.2 broadcast_in_dim.12
  172.7 0.2 constant_dynamic-update-slice_fusion.3
  172.9 0.1 collective-permute-start.1
  173.0 2.7 collective-permute-start.2
  175.6 8.6 %collective-permute-done.1 = bf16[96,2048]{1,0:T(8,128)(2,1)S(1)} collective-permute-done((bf16[96,2048]{1,0:T(8,128)(2,1)S(1)}, bf16[96,2048]{1,0:T(8,128)(2,1)S(1)}, u32[]{:S(2)}, u32[]{:S(2)}) %collective-permute-start.1) | collective-permute-done | bytes 393248 | tf_op jit(solution)/shard_map/ppermute | solution.py:26
  184.3 10.2 %collective-permute-done.3 = bf16[96,2048]{1,0:T(8,128)(2,1)S(1)} collective-permute-done((bf16[96,2048]{1,0:T(8,128)(2,1)S(1)}, bf16[96,2048]{1,0:T(8,128)(2,1)S(1)}, u32[]{:S(2)}, u32[]{:S(2)}) %collective-permute-start.3) | collective-permute-done | bytes 393248 | tf_op jit(solution)/shard_map/ppermute | solution.py:26
  194.6 7.6 %all-gather.7.cloned.1.call-done = bf16[2048,2048]{1,0:T(8,128)(2,1)} async-done(((bf16[64,2048]{1,0:T(8,128)(2,1)}), bf16[2048,2048]{1,0:T(8,128)(2,1)}) %all-gather.7.cloned.1.call-update) | async-done | bytes 8388624 | tf_op jit(solution)/shard_map/all_gather | solution.py:165
  202.2 8.5 %fusion.49 = f32[384,2048]{1,0:T(8,128)} fusion(bf16[384,2048]{1,0:T(8,128)(2,1)S(1)} %constant_dynamic-update-slice_fusion, bf16[2048,2048]{1,0:T(8,128)(2,1)} %all-gather.7.cloned.1.call-done), kind=kOutput, calls=%fused_computation.82 | convolution fusion | flops 3221225472 | bytes 13107200 | tf_op jit(solution)/shard_map/dot_general | solution.py:163
  210.7 61.8 %all-gather.11.cloned.1.call-done = bf16[2048,2048]{1,0:T(8,128)(2,1)} async-done(((bf16[64,2048]{1,0:T(8,128)(2,1)}), bf16[2048,2048]{1,0:T(8,128)(2,1)}) %all-gather.11.cloned.1.call-update) | async-done | bytes 8388624 | tf_op jit(solution)/shard_map/all_gather | solution.py:170
  272.6 70.6 %all-gather.9.cloned.1.call-done = bf16[2048,2048]{1,0:T(8,128)(2,1)} async-done(((bf16[64,2048]{1,0:T(8,128)(2,1)}), bf16[2048,2048]{1,0:T(8,128)(2,1)}) %all-gather.9.cloned.1.call-update) | async-done | bytes 8388624 | tf_op jit(solution)/shard_map/all_gather | solution.py:166
  343.2 15.9 %fusion.10 = f32[384,2048]{1,0:T(8,128)} fusion(bf16[2048,2048]{1,0:T(8,128)(2,1)} %all-gather.11.cloned.1.call-done, f32[384,2048]{1,0:T(8,128)} %fusion.49, bf16[384,2048]{1,0:T(8,128)(2,1)} %copy-done.3, bf16[2048,2048]{1,0:T(8,128)(2,1)} %all-gather.9.cloned.1.call-done), kind=kOutput, calls=%fused_computation.16 | convolution fusion | flops 6447169536 | bytes 24641536 | tf_op jit(solution)/shard_map/dot_general | solution.py:168
  359.1 40.0 %reduce-scatter.5.cloned.1.call-done = f32[96,2048]{1,0:T(8,128)} async-done(((f32[384,2048]{1,0:T(8,128)}), f32[96,2048]{1,0:T(8,128)}) %reduce-scatter.5.cloned.1.call-update) | async-done | bytes 786448 | tf_op jit(solution)/shard_map/reduce_scatter | solution.py:174
  399.1 2.0 fusion.26
  (36 shorter events, 0.2 us)
Async XLA Ops:
  7.4 98.9 %copy-start = (bf16[512,2048]{1,0:T(8,128)(2,1)S(1)}, bf16[512,2048]{1,0:T(8,128)(2,1)}, u32[]{:S(2)}) copy-start(bf16[512,2048]{1,0:T(8,128)(2,1)} %param.20) | copy-start | bytes 6291460
  7.4 70.5 %all-gather.5.cloned.1.call-start = ((), (), s32[]{:S(2)}) async-start(), calls=%async_computation.3 | async-start | bytes 1966080 | tf_op jit(solution)/shard_map/all_gather | solution.py:134
  9.1 36.3 %collective-permute-start = (bf16[128,4096]{0,1:T(8,128)(2,1)S(1)}, bf16[128,4096]{0,1:T(8,128)(2,1)}, u32[]{:S(2)}, u32[]{:S(2)}) collective-permute-start(bf16[128,4096]{0,1:T(8,128)(2,1)S(1)} %copy.71), channel_id=1, source_target_pairs={{0,128},{128,0},{1,129},{129,1},{2,130},{130,2},{3,131},{131,3},{4... | collective-permute-start | bytes 3145736 | tf_op jit(solution)/shard_map/ppermute | solution.py:48
  56.2 14.5 %all-to-all-start = ((bf16[128,2,2048]{0,1,2:T(2,128)(2,1)}), bf16[128,2,2048]{0,1,2:T(2,128)(2,1)S(1)}, u32[]{:S(2)}, u32[]{:S(2)}) async-start(bf16[128,2,2048]{0,1,2:T(2,128)(2,1)} %copy.73), calls=%async_computation | async-start | bytes 2097152 | tf_op jit(solution)/shard_map/all_to_all | solution.py:129
  60.9 109.9 %reduce-scatter.3.cloned.1.call-start = ((), (), s32[]{:S(2)}) async-start(), calls=%async_computation.4 | async-start | bytes 3932160 | tf_op jit(solution)/shard_map/reduce_scatter | solution.py:152
  77.9 3.8 copy-start.2
  98.7 2.3 copy-start.5
  98.7 2.3 copy-start.6
  101.4 1.0 copy-start.9
  102.4 2.7 copy-start.7
  102.4 2.7 copy-start.8
  109.0 61.8 %copy-start.4 = (bf16[96,2048]{1,0:T(8,128)(2,1)S(1)}, bf16[96,2048]{1,0:T(8,128)(2,1)}, u32[]{:S(2)}) copy-start(bf16[96,2048]{1,0:T(8,128)(2,1)} %param.12) | copy-start | bytes 1179652
  109.0 93.2 %all-gather.7.cloned.1.call-start = ((), (), s32[]{:S(2)}) async-start(), calls=%async_computation.5 | async-start | bytes 8650752 | tf_op jit(solution)/shard_map/all_gather | solution.py:165
  109.6 163.0 %all-gather.11.cloned.1.call-start = ((), (), s32[]{:S(2)}) async-start(), calls=%async_computation.7 | async-start | bytes 8650752 | tf_op jit(solution)/shard_map/all_gather | solution.py:170
  110.2 233.0 %all-gather.9.cloned.1.call-start = ((), (), s32[]{:S(2)}) async-start(), calls=%async_computation.6 | async-start | bytes 8650752 | tf_op jit(solution)/shard_map/all_gather | solution.py:166
  110.8 288.3 %reduce-scatter.5.cloned.1.call-start = ((), (), s32[]{:S(2)}) async-start(), calls=%async_computation.8 | async-start | bytes 3932160 | tf_op jit(solution)/shard_map/reduce_scatter | solution.py:174
  172.9 11.3 %collective-permute-start.1 = (bf16[96,2048]{1,0:T(8,128)(2,1)S(1)}, bf16[96,2048]{1,0:T(8,128)(2,1)S(1)}, u32[]{:S(2)}, u32[]{:S(2)}) collective-permute-start(bf16[96,2048]{1,0:T(8,128)(2,1)S(1)} %get-tuple-element.6), channel_id=1, source_target_pairs={{0,1},{1,2},{2,3},{3,0},{4,5},{5,6},{6,7},{7,4},{8,9},{9,10},{10,1... | collective-permute-start | bytes 1179656 | tf_op jit(solution)/shard_map/ppermute | solution.py:26
  173.0 11.3 %collective-permute-start.2 = (bf16[96,2048]{1,0:T(8,128)(2,1)S(1)}, bf16[96,2048]{1,0:T(8,128)(2,1)S(1)}, u32[]{:S(2)}, u32[]{:S(2)}) collective-permute-start(bf16[96,2048]{1,0:T(8,128)(2,1)S(1)} %get-tuple-element.6), channel_id=1, source_target_pairs={{0,3},{1,0},{2,1},{3,2},{4,7},{5,4},{6,5},{7,6},{8,11},{9,8},{10,9... | collective-permute-start | bytes 1179656 | tf_op jit(solution)/shard_map/ppermute | solution.py:33
  184.2 10.3 %collective-permute-start.3 = (bf16[96,2048]{1,0:T(8,128)(2,1)S(1)}, bf16[96,2048]{1,0:T(8,128)(2,1)S(1)}, u32[]{:S(2)}, u32[]{:S(2)}) collective-permute-start(bf16[96,2048]{1,0:T(8,128)(2,1)S(1)} %collective-permute-done.1), channel_id=1, source_target_pairs={{0,1},{1,2},{2,3},{3,0},{4,5},{5,6},{6,7},{7,4},{8,9},{9,10},{10,1... | collective-permute-start | bytes 1179656 | tf_op jit(solution)/shard_map/ppermute | solution.py:26
  194.6 16.2 %copy-start.3 = (bf16[384,2048]{1,0:T(8,128)(2,1)}, bf16[384,2048]{1,0:T(8,128)(2,1)S(1)}, u32[]{:S(2)}) copy-start(bf16[384,2048]{1,0:T(8,128)(2,1)S(1)} %constant_dynamic-update-slice_fusion) | copy-start | bytes 4718596
  343.2 57.8 %copy-start.1 = (bf16[512,2048]{1,0:T(8,128)(2,1)S(1)}, bf16[512,2048]{1,0:T(8,128)(2,1)}, u32[]{:S(2)}) copy-start(bf16[512,2048]{1,0:T(8,128)(2,1)} %param.20) | copy-start | bytes 6291460
Sparse Core Ops, SparseCore 0:
  17.1 27.0 all-gather.4
  109.1 61.6 reduce-scatter.2
  359.2 39.8 reduce-scatter.4
Sparse Core Ops, SparseCore 1:
  111.4 90.8 all-gather.6
  203.9 68.6 all-gather.10
  274.3 68.9 all-gather.8
